TPU v7x, 32 devices: a whole 2x2x4 slice. The times are simulated.
32 devices in a mesh: fsdp: 4 (over x, core), ctx: 8 (over z, y).
Axes of the slice: x: 2, y: 2, z: 4, core: 2. Of those that a mesh axis runs over, the one named last changes fastest.
Arguments:
- tokens: bfloat16 [4, 2048, 1024], P('fsdp', 'ctx'), may hold values from -6 to 6
- out_grad: bfloat16 [4, 2048, 1024], P('fsdp', 'ctx'), may hold values from -6 to 6
- slot_block: int32 [4, 16], P('fsdp'), may hold values from 0 to 15, as said below
- w_attend: bfloat16 [1024, 3072], P('fsdp'), may hold values from -0.1875 to 0.1875
- w_mixing: bfloat16 [1024, 1024], P('fsdp'), may hold values from -1 to 1
- w_expand: bfloat16 [1024, 4096], P('fsdp'), may hold values from -0.1875 to 0.1875
- w_shrink: bfloat16 [4096, 1024], P('fsdp'), may hold values from -0.09375 to 0.09375
- w_norms: bfloat16 [4, 1024], P(None, 'fsdp'), may hold values from -1.2 to 1.4
- first_attend: float32 [1024, 3072], P('fsdp'), may hold values from -24 to 24
- first_mixing: float32 [1024, 1024], P('fsdp'), may hold values from -24 to 24
- first_expand: float32 [1024, 4096], P('fsdp'), may hold values from -24 to 24
- first_shrink: float32 [4096, 1024], P('fsdp'), may hold values from -24 to 24
- first_norms: float32 [4, 1024], P(None, 'fsdp'), may hold values from -24 to 24
- second_attend: float32 [1024, 3072], P('fsdp'), may hold values from 0.5 to 8
- second_mixing: float32 [1024, 1024], P('fsdp'), may hold values from 0.5 to 8
- second_expand: float32 [1024, 4096], P('fsdp'), may hold values from 0.5 to 8
- second_shrink: float32 [4096, 1024], P('fsdp'), may hold values from 0.5 to 8
- second_norms: float32 [4, 1024], P(None, 'fsdp'), may hold values from 0.5 to 8
Outputs:
- layer_out: bfloat16 [4, 2048, 1024], P('fsdp', 'ctx')
- tokens_grad: float32 [4, 2048, 1024], P('fsdp', 'ctx')
- grad_attend: float32 [1024, 3072], P('fsdp')
- update_attend: float32 [1024, 3072], P('fsdp')
- first_new_attend: float32 [1024, 3072], P('fsdp')
- second_new_attend: float32 [1024, 3072], P('fsdp')
- grad_mixing: float32 [1024, 1024], P('fsdp')
- update_mixing: float32 [1024, 1024], P('fsdp')
- first_new_mixing: float32 [1024, 1024], P('fsdp')
- second_new_mixing: float32 [1024, 1024], P('fsdp')
- grad_expand: float32 [1024, 4096], P('fsdp')
- update_expand: float32 [1024, 4096], P('fsdp')
- first_new_expand: float32 [1024, 4096], P('fsdp')
- second_new_expand: float32 [1024, 4096], P('fsdp')
- grad_shrink: float32 [4096, 1024], P('fsdp')
- update_shrink: float32 [4096, 1024], P('fsdp')
- first_new_shrink: float32 [4096, 1024], P('fsdp')
- second_new_shrink: float32 [4096, 1024], P('fsdp')
- grad_norms: float32 [4, 1024], P(None, 'fsdp')
- update_norms: float32 [4, 1024], P(None, 'fsdp')
- first_new_norms: float32 [4, 1024], P(None, 'fsdp')
- second_new_norms: float32 [4, 1024], P(None, 'fsdp')
Inputs may be any that keep to these rules, and one draw needn't show every extreme that they name: `slot_block`: in each row every block number appears once, and slots 2i and 2i+1 hold two blocks whose numbers add up to 15.
All inputs are finite; a program needn't handle non-finite values.
Results may differ from a plain program's by a relative error of at most 0.025.
Values may be sent and summed in bfloat16 or wider, within the bound.
A program may use at most 256 MiB of HBM per device.

v0:
```python
import math
import jax
import jax.numpy as jnp
from jax import lax
from jax.sharding import PartitionSpec as P

HD = 64
HGROUP = 2
STEP_COUNT = 10
EPS_NORM = 1e-05
NEG = -1e30
BETA_ONE = 0.9
BETA_TWO = 0.999
LEARN = 0.02
DECAY = 0.1
EPS_ADAM = 1e-08
CUBIC = 0.044715
ROOT_TWO_PI = math.sqrt(2.0 / math.pi)


def layer_norm(values, gain, shift):
    center = values - jnp.mean(values, axis=-1, keepdims=True)
    spread = jnp.mean(center * center, axis=-1, keepdims=True)
    return center * lax.rsqrt(spread + EPS_NORM) * gain + shift


def gelu(values):
    cube = values * values * values
    return 0.5 * values * (1.0 + jnp.tanh(ROOT_TWO_PI * (values + CUBIC * cube)))


def positions(slots, block):
    offsets = jnp.arange(block, dtype=jnp.int32)
    placed = slots[:, :, None] * block + offsets[None, None, :]
    return placed.reshape(slots.shape[0], slots.shape[1] * block)


def adam_step(weight, grad, first, second):
    first_new = BETA_ONE * first + (1.0 - BETA_ONE) * grad
    second_new = BETA_TWO * second + (1.0 - BETA_TWO) * grad * grad
    mean_hat = first_new / (1.0 - BETA_ONE**STEP_COUNT)
    square_hat = second_new / (1.0 - BETA_TWO**STEP_COUNT)
    update = -LEARN * (
        mean_hat / (jnp.sqrt(square_hat) + EPS_ADAM) + DECAY * weight.astype(jnp.float32)
    )
    return (update, first_new, second_new)


def shards(
    tokens,
    out_grad,
    slot_block,
    w_attend,
    w_mixing,
    w_expand,
    w_shrink,
    w_norms,
    first_attend,
    first_mixing,
    first_expand,
    first_shrink,
    first_norms,
    second_attend,
    second_mixing,
    second_expand,
    second_shrink,
    second_norms,
):
    whole_attend, whole_mixing, whole_expand, whole_shrink, whole_norms = (
        lax.all_gather(w_attend, "fsdp", axis=0, tiled=True),
        lax.all_gather(w_mixing, "fsdp", axis=0, tiled=True),
        lax.all_gather(w_expand, "fsdp", axis=0, tiled=True),
        lax.all_gather(w_shrink, "fsdp", axis=0, tiled=True),
        lax.all_gather(w_norms, "fsdp", axis=1, tiled=True),
    )
    seqs, local, width = tokens.shape
    block = local // 2
    length = slot_block.shape[1] * block
    total_rows = seqs * local
    heads = width // HD
    group_width = HGROUP * HD
    scale = 1.0 / math.sqrt(HD)
    norm_values = whole_norms.astype(jnp.float32)
    owned = lax.dynamic_slice_in_dim(slot_block, 2 * lax.axis_index("ctx"), 2, 1)
    query_place = positions(owned, block)
    key_place = positions(slot_block, block)
    allowed = key_place[:, None, None, :] <= query_place[:, None, :, None]
    start = tokens.reshape(total_rows, width).astype(jnp.float32)
    normed, norm_back = jax.vjp(layer_norm, start, norm_values[0], norm_values[1])
    normed_low = normed.astype(jnp.bfloat16)
    joint = jnp.dot(normed_low, whole_attend, preferred_element_type=jnp.float32).astype(
        jnp.bfloat16
    )
    query = joint[:, :width].reshape(seqs, local, width)
    keys_own = joint[:, width : 2 * width].reshape(seqs, local, width)
    values_own = joint[:, 2 * width :].reshape(seqs, local, width)
    keys, values = (
        lax.all_gather(keys_own, "ctx", axis=1, tiled=True),
        lax.all_gather(values_own, "ctx", axis=1, tiled=True),
    )

    def group_scores(index):
        offset = index * group_width
        query_group = lax.dynamic_slice_in_dim(query, offset, group_width, 2).reshape(
            seqs, local, HGROUP, HD
        )
        key_group = lax.dynamic_slice_in_dim(keys, offset, group_width, 2).reshape(
            seqs, length, HGROUP, HD
        )
        value_group = lax.dynamic_slice_in_dim(values, offset, group_width, 2).reshape(
            seqs, length, HGROUP, HD
        )
        raw = (
            jnp.einsum(
                "sqhd,skhd->shqk", query_group, key_group, preferred_element_type=jnp.float32
            )
            * scale
        )
        return (jnp.where(allowed, raw, NEG), query_group, key_group, value_group)

    def forward_group(index, state):
        mixed_buffer, totals_buffer = state
        masked, query_group, key_group, value_group = group_scores(index)
        top = jnp.max(masked, axis=-1, keepdims=True)
        total = top + jnp.log(jnp.sum(jnp.exp(masked - top), axis=-1, keepdims=True))
        probs = jnp.exp(masked - total).astype(jnp.bfloat16)
        result = jnp.einsum(
            "shqk,skhd->sqhd", probs, value_group, preferred_element_type=jnp.float32
        )
        result = result.reshape(seqs, local, group_width).astype(jnp.bfloat16)
        mixed_buffer = lax.dynamic_update_slice_in_dim(mixed_buffer, result, index * group_width, 2)
        totals_buffer = lax.dynamic_update_slice_in_dim(
            totals_buffer, total[..., 0], index * HGROUP, 1
        )
        return (mixed_buffer, totals_buffer)

    mixed, totals = lax.fori_loop(
        0,
        heads // HGROUP,
        forward_group,
        (
            jnp.zeros((seqs, local, width), jnp.bfloat16),
            jnp.zeros((seqs, heads, local), jnp.float32),
        ),
    )
    mixed_rows = mixed.reshape(total_rows, width)
    middle = start + jnp.dot(mixed_rows, whole_mixing, preferred_element_type=jnp.float32)
    normed_two, norm_two_back = jax.vjp(layer_norm, middle, norm_values[2], norm_values[3])
    normed_two_low = normed_two.astype(jnp.bfloat16)
    expanded = jnp.dot(normed_two_low, whole_expand, preferred_element_type=jnp.float32)
    activated, gelu_back = jax.vjp(gelu, expanded)
    activated_low = activated.astype(jnp.bfloat16)
    result_rows = middle + jnp.dot(activated_low, whole_shrink, preferred_element_type=jnp.float32)
    layer_out = result_rows.reshape(seqs, local, width).astype(jnp.bfloat16)
    incoming = out_grad.reshape(total_rows, width)
    grad_shrink = jnp.dot(activated_low.T, incoming, preferred_element_type=jnp.float32)
    grad_activated = jnp.dot(incoming, whole_shrink.T, preferred_element_type=jnp.float32).astype(
        jnp.bfloat16
    )
    grad_expanded = gelu_back(grad_activated.astype(jnp.float32))[0].astype(jnp.bfloat16)
    grad_expand = jnp.dot(normed_two_low.T, grad_expanded, preferred_element_type=jnp.float32)
    grad_normed_two = jnp.dot(grad_expanded, whole_expand.T, preferred_element_type=jnp.float32)
    grad_middle_norm, grad_gain_two, grad_shift_two = norm_two_back(grad_normed_two)
    grad_middle = incoming.astype(jnp.float32) + grad_middle_norm
    grad_branch = grad_middle.astype(jnp.bfloat16)
    grad_mixing = jnp.dot(mixed_rows.T, grad_branch, preferred_element_type=jnp.float32)
    grad_mixed = jnp.dot(grad_branch, whole_mixing.T, preferred_element_type=jnp.float32)
    grad_mixed = grad_mixed.astype(jnp.bfloat16).reshape(seqs, local, width)

    def backward_group(index, state):
        grad_query, grad_keys, grad_values = state
        offset = index * group_width
        masked, query_group, key_group, value_group = group_scores(index)
        total = lax.dynamic_slice_in_dim(totals, index * HGROUP, HGROUP, 1)
        probs = jnp.exp(masked - total[..., None])
        grad_group = lax.dynamic_slice_in_dim(grad_mixed, offset, group_width, 2).reshape(
            seqs, local, HGROUP, HD
        )
        grad_probs = jnp.einsum(
            "sqhd,skhd->shqk", grad_group, value_group, preferred_element_type=jnp.float32
        )
        grad_scores = probs * (grad_probs - jnp.sum(probs * grad_probs, axis=-1, keepdims=True))
        grad_scores = grad_scores.astype(jnp.bfloat16)
        part_query = (
            jnp.einsum(
                "shqk,skhd->sqhd", grad_scores, key_group, preferred_element_type=jnp.float32
            )
            * scale
        )
        part_keys = (
            jnp.einsum(
                "shqk,sqhd->skhd", grad_scores, query_group, preferred_element_type=jnp.float32
            )
            * scale
        )
        part_values = jnp.einsum(
            "shqk,sqhd->skhd",
            probs.astype(jnp.bfloat16),
            grad_group,
            preferred_element_type=jnp.float32,
        )
        grad_query = lax.dynamic_update_slice_in_dim(
            grad_query, part_query.reshape(seqs, local, group_width), offset, 2
        )
        grad_keys = lax.dynamic_update_slice_in_dim(
            grad_keys, part_keys.reshape(seqs, length, group_width), offset, 2
        )
        grad_values = lax.dynamic_update_slice_in_dim(
            grad_values, part_values.reshape(seqs, length, group_width), offset, 2
        )
        return (grad_query, grad_keys, grad_values)

    grad_query, grad_keys_all, grad_values_all = lax.fori_loop(
        0,
        heads // HGROUP,
        backward_group,
        (
            jnp.zeros((seqs, local, width), jnp.float32),
            jnp.zeros((seqs, length, width), jnp.float32),
            jnp.zeros((seqs, length, width), jnp.float32),
        ),
    )
    grad_keys, grad_values = (
        lax.psum_scatter(
            grad_keys_all.astype(jnp.bfloat16), "ctx", scatter_dimension=1, tiled=True
        ).astype(jnp.float32),
        lax.psum_scatter(
            grad_values_all.astype(jnp.bfloat16), "ctx", scatter_dimension=1, tiled=True
        ).astype(jnp.float32),
    )
    grad_joint = jnp.concatenate(
        [
            grad_query.astype(jnp.bfloat16),
            grad_keys.astype(jnp.bfloat16),
            grad_values.astype(jnp.bfloat16),
        ],
        axis=2,
    ).reshape(total_rows, 3 * width)
    grad_attend = jnp.dot(normed_low.T, grad_joint, preferred_element_type=jnp.float32)
    grad_normed = jnp.dot(grad_joint, whole_attend.T, preferred_element_type=jnp.float32)
    grad_start_norm, grad_gain_one, grad_shift_one = norm_back(grad_normed)
    tokens_grad = (grad_middle + grad_start_norm).reshape(seqs, local, width)
    grad_norms = jnp.stack([grad_gain_one, grad_shift_one, grad_gain_two, grad_shift_two])
    owned_attend, owned_mixing, owned_expand, owned_shrink, owned_norms = (
        lax.psum_scatter(
            grad_attend.astype(jnp.bfloat16), "fsdp", scatter_dimension=0, tiled=True
        ).astype(jnp.float32),
        lax.psum_scatter(
            grad_mixing.astype(jnp.bfloat16), "fsdp", scatter_dimension=0, tiled=True
        ).astype(jnp.float32),
        lax.psum_scatter(
            grad_expand.astype(jnp.bfloat16), "fsdp", scatter_dimension=0, tiled=True
        ).astype(jnp.float32),
        lax.psum_scatter(
            grad_shrink.astype(jnp.bfloat16), "fsdp", scatter_dimension=0, tiled=True
        ).astype(jnp.float32),
        lax.psum_scatter(
            grad_norms.astype(jnp.bfloat16), "fsdp", scatter_dimension=1, tiled=True
        ).astype(jnp.float32),
    )
    sum_attend, sum_mixing, sum_expand, sum_shrink, sum_norms = (
        lax.psum(owned_attend.astype(jnp.bfloat16), "ctx").astype(jnp.float32),
        lax.psum(owned_mixing.astype(jnp.bfloat16), "ctx").astype(jnp.float32),
        lax.psum(owned_expand.astype(jnp.bfloat16), "ctx").astype(jnp.float32),
        lax.psum(owned_shrink.astype(jnp.bfloat16), "ctx").astype(jnp.float32),
        lax.psum(owned_norms.astype(jnp.bfloat16), "ctx").astype(jnp.float32),
    )
    update_attend, first_new_attend, second_new_attend = adam_step(
        w_attend, sum_attend, first_attend, second_attend
    )
    update_mixing, first_new_mixing, second_new_mixing = adam_step(
        w_mixing, sum_mixing, first_mixing, second_mixing
    )
    update_expand, first_new_expand, second_new_expand = adam_step(
        w_expand, sum_expand, first_expand, second_expand
    )
    update_shrink, first_new_shrink, second_new_shrink = adam_step(
        w_shrink, sum_shrink, first_shrink, second_shrink
    )
    update_norms, first_new_norms, second_new_norms = adam_step(
        w_norms, sum_norms, first_norms, second_norms
    )
    return (
        layer_out,
        tokens_grad,
        sum_attend,
        update_attend,
        first_new_attend,
        second_new_attend,
        sum_mixing,
        update_mixing,
        first_new_mixing,
        second_new_mixing,
        sum_expand,
        update_expand,
        first_new_expand,
        second_new_expand,
        sum_shrink,
        update_shrink,
        first_new_shrink,
        second_new_shrink,
        sum_norms,
        update_norms,
        first_new_norms,
        second_new_norms,
    )


def solution(mesh):
    return jax.shard_map(
        shards,
        mesh=mesh,
        in_specs=(
            P("fsdp", "ctx", None),
            P("fsdp", "ctx", None),
            P("fsdp", None),
            P("fsdp", None),
            P("fsdp", None),
            P("fsdp", None),
            P("fsdp", None),
            P(None, "fsdp"),
            P("fsdp", None),
            P("fsdp", None),
            P("fsdp", None),
            P("fsdp", None),
            P(None, "fsdp"),
            P("fsdp", None),
            P("fsdp", None),
            P("fsdp", None),
            P("fsdp", None),
            P(None, "fsdp"),
        ),
        out_specs=(
            P("fsdp", "ctx", None),
            P("fsdp", "ctx", None),
            P("fsdp", None),
            P("fsdp", None),
            P("fsdp", None),
            P("fsdp", None),
            P("fsdp", None),
            P("fsdp", None),
            P("fsdp", None),
            P("fsdp", None),
            P("fsdp", None),
            P("fsdp", None),
            P("fsdp", None),
            P("fsdp", None),
            P("fsdp", None),
            P("fsdp", None),
            P("fsdp", None),
            P("fsdp", None),
            P(None, "fsdp"),
            P(None, "fsdp"),
            P(None, "fsdp"),
            P(None, "fsdp"),
        ),
        check_vma=False,
    )
```

profile of v0, /device:TPU:0, one launch (start us, length us, event | category | flops | bytes accessed | tf_op | source)
XLA Modules:
  0.0 1199.6 jit_solution(6608566212357250092)
XLA Ops:
  8.0 6.3 all_gather.21
  16.8 41.9 %all-gather.9.cloned.1.call-done = bf16[1024,3072]{1,0:T(8,128)(2,1)} async-done(((bf16[256,3072]{1,0:T(8,128)(2,1)}), bf16[1024,3072]{1,0:T(8,128)(2,1)}) %all-gather.9.cloned.1.call-update) | async-done | bytes 6291472 | tf_op jit(solution)/shard_map/all_gather | solution.py:70
  58.7 4.9 convolution_convert_fusion.4
  67.8 70.6 %all-gather.17.cloned.1.call-done = bf16[2048,1024]{1,0:T(8,128)(2,1)} async-done(((bf16[256,1024]{1,0:T(8,128)(2,1)}), bf16[2048,1024]{1,0:T(8,128)(2,1)}) %all-gather.17.cloned.1.call-update) | async-done | bytes 4194320 | tf_op jit(solution)/shard_map/all_gather | solution.py:99
  138.4 6.4 copy.47
  144.8 68.0 %all-gather.19.cloned.1.call-done = bf16[2048,1024]{1,0:T(8,128)(2,1)} async-done(((bf16[256,1024]{1,0:T(8,128)(2,1)}), bf16[2048,1024]{1,0:T(8,128)(2,1)}) %all-gather.19.cloned.1.call-update) | async-done | bytes 4194320 | tf_op jit(solution)/shard_map/all_gather | solution.py:98
  212.8 6.4 copy.49
  219.3 74.3 %while.34 = (s32[]{:T(128)}, bf16[1,256,1024]{1,2,0:T(8,128)(2,1)S(1)}, f32[1,16,256]{2,1,0:T(8,128)S(1)}, bf16[1,2048,1024]{1,2,0:T(8,128)(2,1)}, bf16[1,256,10...) while((s32[]{:T(128)}, ...), condition=%wide.region_5.6_spmd.clone, body=%wide.region_2.5_spmd.clone.sunk | while | flops 276332032 | bytes 33973524 | solution.py:137
  221.0 3.0 fusion.120
  224.1 3.1 exponential_reduce_fusion.2
  230.2 3.0 fusion.120
  233.2 3.1 exponential_reduce_fusion.2
  239.3 3.0 fusion.120
  242.3 3.6 exponential_reduce_fusion.2
  249.6 3.0 fusion.120
  258.8 3.0 fusion.120
  267.9 3.0 fusion.120
  270.9 3.1 exponential_reduce_fusion.2
  297.1 7.9 fusion.64
  305.0 49.5 %all-gather.15.cloned.1.call-done = bf16[4096,1024]{1,0:T(8,128)(2,1)} async-done(((bf16[1024,1024]{1,0:T(8,128)(2,1)}), bf16[4096,1024]{1,0:T(8,128)(2,1)}) %all-gather.15.cloned.1.call-update) | async-done | bytes 8388624 | tf_op jit(solution)/shard_map/all_gather | solution.py:73
  354.6 8.7 fusion.17
  375.0 120.1 %while.35 = (s32[]{:T(128)}, bf16[1,256,1024]{1,2,0:T(8,128)(2,1)}, bf16[1,2048,1024]{1,2,0:T(8,128)(2,1)}, bf16[1,2048,1024]{1,2,0:T(8,128)(2,1)}, bf16[1,2048,...) while((s32[]{:T(128)}, bf16[1,256,1024]{1,2,0:T(8,128)(2,1)}, ...), condition=%wide.region_12.13_spmd.clone, body=%wide.region_10.0_spmd.clone.sunk | while | flops 681639424 | bytes 56970552 | solution.py:213
  382.1 4.0 multiply_reduce_fusion.5
  397.2 4.0 multiply_reduce_fusion.5
  412.2 4.0 multiply_reduce_fusion.5
  427.2 4.0 multiply_reduce_fusion.5
  442.2 4.0 multiply_reduce_fusion.5
  457.2 4.0 multiply_reduce_fusion.5
  472.2 4.0 multiply_reduce_fusion.5
  487.2 4.0 multiply_reduce_fusion.5
  496.2 3.1 convolution_convert_fusion.5
  499.5 7.3 convolution_convert_fusion.1
  507.9 8.5 convolution_convert_fusion
  516.4 67.2 %reduce-scatter.12.cloned.1.call-done = bf16[1,256,1024]{1,2,0:T(8,128)(2,1)} async-done(((bf16[1,2048,1024]{1,2,0:T(8,128)(2,1)}), bf16[1,256,1024]{1,2,0:T(8,128)(2,1)}) %reduce-scatter.12.cloned.1.call-update) | async-done | bytes 524304 | tf_op jit(solution)/shard_map/reduce_scatter | solution.py:227
  583.6 92.7 %reduce-scatter.10.cloned.1.call-done = bf16[1,256,1024]{1,2,0:T(8,128)(2,1)} async-done(((bf16[1,2048,1024]{1,2,0:T(8,128)(2,1)}), bf16[1,256,1024]{1,2,0:T(8,128)(2,1)}) %reduce-scatter.10.cloned.1.call-update) | async-done | bytes 524304 | tf_op jit(solution)/shard_map/reduce_scatter | solution.py:224
  676.4 6.0 convolution_convert_fusion.2
  682.5 5.4 fusion.35
  690.7 20.0 %reduce-scatter.16.cloned.1.call-done = bf16[256,1024]{1,0:T(8,128)(2,1)} async-done(((bf16[1024,1024]{1,0:T(8,128)(2,1)}), bf16[256,1024]{1,0:T(8,128)(2,1)}) %reduce-scatter.16.cloned.1.call-update) | async-done | bytes 524304 | tf_op jit(solution)/shard_map/reduce_scatter | solution.py:248
  710.7 74.4 %reduce-scatter.18.cloned.1.call-done = bf16[256,4096]{1,0:T(8,128)(2,1)} async-done(((bf16[1024,4096]{1,0:T(8,128)(2,1)}), bf16[256,4096]{1,0:T(8,128)(2,1)}) %reduce-scatter.18.cloned.1.call-update) | async-done | bytes 2097168 | tf_op jit(solution)/shard_map/reduce_scatter | solution.py:251
  785.0 74.3 %reduce-scatter.20.cloned.1.call-done = bf16[1024,1024]{1,0:T(8,128)(2,1)} async-done(((bf16[4096,1024]{1,0:T(8,128)(2,1)}), bf16[1024,1024]{1,0:T(8,128)(2,1)}) %reduce-scatter.20.cloned.1.call-update) | async-done | bytes 2097168 | tf_op jit(solution)/shard_map/reduce_scatter | solution.py:254
  859.4 60.9 %reduce-scatter.14.cloned.1.call-done = bf16[256,3072]{1,0:T(8,128)(2,1)} async-done(((bf16[1024,3072]{1,0:T(8,128)(2,1)}), bf16[256,3072]{1,0:T(8,128)(2,1)}) %reduce-scatter.14.cloned.1.call-update) | async-done | bytes 1572880 | tf_op jit(solution)/shard_map/reduce_scatter | solution.py:245
  920.4 8.3 fusion.28
  930.2 13.3 %reduce-scatter.22.cloned.1.call-done = bf16[256,4]{1,0:T(8,128)(2,1)} async-done(((bf16[1024,4]{1,0:T(8,128)(2,1)}), bf16[256,4]{1,0:T(8,128)(2,1)}) %reduce-scatter.22.cloned.1.call-update) | async-done | bytes 2064
  944.4 21.8 %psum.39 = bf16[4,256]{1,0:T(4,128)(2,1)S(1)} all-reduce(bf16[4,256]{1,0:T(4,128)(2,1)S(1)} %copy.55), channel_id=1, replica_groups=mesh['fsdp'=4,'ctx'=8] {'ctx'}, use_global_device_ids=true, to_apply=%region_30.31 | all-reduce | flops 1024 | bytes 4096 | tf_op jit(solution)/shard_map/psum | solution.py:266
  966.8 196.3 %all-reduce.3.cloned.1.call-done = (bf16[256,3072]{1,0:T(8,128)(2,1)}, bf16[256,1024]{1,0:T(8,128)(2,1)}, bf16[256,4096]{1,0:T(8,128)(2,1)}, bf16[1024,1024]{1,0:T(8,128)(2,1)}) async-done(((bf16[256,3072]{1,0:T(8,128)(2,1)}, bf16[256,1024]{1,0:T(8,128)(2,1)}, bf16[256,4096]{1,0:T(8,128)(2,1)}, bf16[1024,1024]{1,0:T(8,128)(2,1)}), (bf16[256,3072]{1,0:T(8,128)(2,1)}, bf16[256,1024]{1,0:T(8,128)(2,1)}, ...) | async-done | bytes 6291472 | tf_op jit(solution)/shard_map/psum | solution.py:262
  1163.2 8.7 add_multiply_fusion.2
  1176.2 9.8 add_multiply_fusion.1
  1186.1 6.8 add_multiply_fusion
  (333 shorter events, 165.2 us)
Async XLA Ops:
  7.2 51.5 %all-gather.9.cloned.1.call-start = ((), (), s32[]{:S(2)}) async-start(), calls=%async_computation.7 | async-start | bytes 7864320 | tf_op jit(solution)/shard_map/all_gather | solution.py:70
  7.9 130.4 %all-gather.17.cloned.1.call-start = ((), (), s32[]{:S(2)}) async-start(), calls=%async_computation.17 | async-start | bytes 4718592 | tf_op jit(solution)/shard_map/all_gather | solution.py:99
  16.8 46.8 %copy-start.27 = (f32[256]{0:T(256)}, f32[256]{0:T(256)S(1)}, u32[]{:S(2)}) copy-start(f32[256]{0:T(256)S(1)} %fusion.34) | copy-start | bytes 3076
  63.6 3.7 copy-start.33
  64.7 148.0 %all-gather.19.cloned.1.call-start = ((), (), s32[]{:S(2)}) async-start(), calls=%async_computation.18 | async-start | bytes 4718592 | tf_op jit(solution)/shard_map/all_gather | solution.py:98
  65.5 228.1 %all-gather.11.cloned.1.call-start = ((), (), s32[]{:S(2)}) async-start(), calls=%async_computation.8 | async-start | bytes 2621440 | tf_op jit(solution)/shard_map/all_gather | solution.py:71
  66.1 231.0 %all-gather.13.cloned.1.call-start = ((), (), s32[]{:S(2)}) async-start(), calls=%async_computation.9 | async-start | bytes 10485760 | tf_op jit(solution)/shard_map/all_gather | solution.py:72
  66.6 287.9 %all-gather.15.cloned.1.call-start = ((), (), s32[]{:S(2)}) async-start(), calls=%async_computation.10 | async-start | bytes 10485760 | tf_op jit(solution)/shard_map/all_gather | solution.py:73
  67.2 516.4 %reduce-scatter.12.cloned.1.call-start = ((), (), s32[]{:S(2)}) async-start(), calls=%async_computation.12 | async-start | bytes 4718592 | tf_op jit(solution)/shard_map/reduce_scatter | solution.py:227
  219.2 75.1 %copy-start.2 = (bf16[1,256,1024]{2,1,0:T(8,128)(2,1)S(1)}, bf16[1,256,1024]{2,1,0:T(8,128)(2,1)}, u32[]{:S(2)}) copy-start(bf16[1,256,1024]{2,1,0:T(8,128)(2,1)} %param.22) | copy-start | bytes 1572868
  242.3 4.7 copy-start
  293.6 11.5 copy-start.6
  297.1 57.5 %copy-start.19 = (bf16[1,256,1024]{2,1,0:T(8,128)(2,1)S(1)}, bf16[1,256,1024]{2,1,0:T(8,128)(2,1)}, u32[]{:S(2)}) copy-start(bf16[1,256,1024]{2,1,0:T(8,128)(2,1)} %param.23) | copy-start | bytes 1572868
  354.6 8.7 copy-start.32
  367.6 7.4 copy-start.22
  382.1 4.0 copy-start.1
  397.1 4.0 copy-start.1
  412.2 4.0 copy-start.1
  427.2 4.0 copy-start.1
  442.2 4.0 copy-start.1
  457.2 4.0 copy-start.1
  472.2 4.0 copy-start.1
  487.2 4.0 copy-start.1
  495.2 181.2 %reduce-scatter.10.cloned.1.call-start = ((), (), s32[]{:S(2)}) async-start(), calls=%async_computation.11 | async-start | bytes 4718592 | tf_op jit(solution)/shard_map/reduce_scatter | solution.py:224
  495.9 214.7 %reduce-scatter.16.cloned.1.call-start = ((), (), s32[]{:S(2)}) async-start(), calls=%async_computation.14 | async-start | bytes 2621440 | tf_op jit(solution)/shard_map/reduce_scatter | solution.py:248
  499.3 285.8 %reduce-scatter.18.cloned.1.call-start = ((), (), s32[]{:S(2)}) async-start(), calls=%async_computation.15 | async-start | bytes 10485760 | tf_op jit(solution)/shard_map/reduce_scatter | solution.py:251
  506.9 352.5 %reduce-scatter.20.cloned.1.call-start = ((), (), s32[]{:S(2)}) async-start(), calls=%async_computation.16 | async-start | bytes 10485760 | tf_op jit(solution)/shard_map/reduce_scatter | solution.py:254
  516.4 160.0 %copy-start.26 = (bf16[1,256,1024]{1,2,0:T(8,128)(2,1)S(1)}, bf16[1,256,1024]{1,2,0:T(8,128)(2,1)}, u32[]{:S(2)}) copy-start(bf16[1,256,1024]{1,2,0:T(8,128)(2,1)} %get-tuple-element.320) | copy-start | bytes 1572868
  516.4 403.9 %reduce-scatter.14.cloned.1.call-start = ((), (), s32[]{:S(2)}) async-start(), calls=%async_computation.13 | async-start | bytes 7864320 | tf_op jit(solution)/shard_map/reduce_scatter | solution.py:245
  682.4 261.1 %reduce-scatter.22.cloned.1.call-start = ((), (), s32[]{:S(2)}) async-start(), calls=%async_computation.19 | async-start | bytes 327680
  682.5 5.5 copy-start.28
  690.4 472.7 %all-reduce.3.cloned.1.call-start = ((), (), s32[]{:S(2)}) async-start(), calls=%async_computation.20 | async-start | bytes 12582912 | tf_op jit(solution)/shard_map/psum | solution.py:262
  920.3 8.3 copy-start.13
  920.3 8.3 copy-start.21
  928.6 37.6 %copy-start.29 = (bf16[4,256]{1,0:T(4,128)(2,1)S(1)}, bf16[4,256]{1,0:T(4,128)(2,1)}, u32[]{:S(2)}) copy-start(bf16[4,256]{1,0:T(4,128)(2,1)} %param.29) | copy-start | bytes 6148
  928.7 37.6 %copy-start.30 = (f32[4,256]{1,0:T(4,128)S(1)}, f32[4,256]{1,0:T(4,128)}, u32[]{:S(2)}) copy-start(f32[4,256]{1,0:T(4,128)} %param.34) | copy-start | bytes 12292
  928.7 37.6 %copy-start.31 = (f32[4,256]{1,0:T(4,128)S(1)}, f32[4,256]{1,0:T(4,128)}, u32[]{:S(2)}) copy-start(f32[4,256]{1,0:T(4,128)} %param.39) | copy-start | bytes 12292
  928.7 234.5 %copy-start.5 = (bf16[256,3072]{1,0:T(8,128)(2,1)S(1)}, bf16[256,3072]{1,0:T(8,128)(2,1)}, u32[]{:S(2)}) copy-start(bf16[256,3072]{1,0:T(8,128)(2,1)} %param.25) | copy-start | bytes 4718596
  1163.1 8.7 copy-start.16
  1163.1 8.7 copy-start.23
  1163.1 8.7 copy-start.24
  1163.2 8.7 copy-start.25
  1163.2 11.2 copy-start.9
  1171.8 4.4 copy-start.8
  1176.2 9.9 copy-start.4
  1176.2 9.9 copy-start.10
  1176.2 9.9 copy-start.11
  1176.2 9.9 copy-start.15
  (14 other events, 35.1 us)
Sparse Core Ops, SparseCore 0:
  9.6 49.0 all-gather.8
  64.9 73.4 all-gather.16
  141.1 71.6 all-gather.18
  214.2 20.8 all-gather.10
  236.5 58.2 all-gather.12
  296.2 58.3 all-gather.14
  495.3 88.2 reduce-scatter.11
  588.3 88.0 reduce-scatter.9
  679.5 31.1 reduce-scatter.15
  713.3 71.7 reduce-scatter.17
  787.6 71.7 reduce-scatter.19
  861.9 58.3 reduce-scatter.13
  923.3 20.0 reduce-scatter.21
  948.4 214.6 all-reduce.2
where the time goes:
time: 1210 us; the launch traced here: 1200 us
  waiting for transfers between devices  833 us (69%)
  matrix products  166 us (14%)
  local copies, waits for them, and re-layouts  87.7 us (7%)
  other arithmetic  68.2 us (6%)
  blocking collectives  28.1 us (2%)
  between operations  14.6 us (1%)
    psum x1, waiting for transfers between devices, shards(): lax.psum(owned_attend.astype(jnp.bfloat16), 'ctx').astype(jnp.float32)  196 us
    reduce_scatter x1, waiting for transfers between devices, shards(): lax.psum_scatter(grad_keys_all.astype(jnp.bfloat16), 'ctx', scatter_dimen...  92.7 us
    reduce_scatter x1, waiting for transfers between devices, shards(): lax.psum_scatter(grad_expand.astype(jnp.bfloat16), 'fsdp', scatter_dimens...  74.4 us
    reduce_scatter x1, waiting for transfers between devices, shards(): lax.psum_scatter(grad_shrink.astype(jnp.bfloat16), 'fsdp', scatter_dimens...  74.3 us
    all_gather x1, waiting for transfers between devices, shards(): lax.all_gather(values_own, 'ctx', axis=1, tiled=True)  70.6 us
    all_gather x1, waiting for transfers between devices, shards(): lax.all_gather(keys_own, 'ctx', axis=1, tiled=True)  68 us
    reduce_scatter x1, waiting for transfers between devices, shards(): lax.psum_scatter(grad_values_all.astype(jnp.bfloat16), 'ctx', scatter_dim...  67.2 us
    reduce_scatter x1, waiting for transfers between devices, shards(): lax.psum_scatter(grad_attend.astype(jnp.bfloat16), 'fsdp', scatter_dimens...  60.9 us
  transfers between devices with their start and end apart: 14, of which 12 were waited for; matrix products, arithmetic and copies ran while one was open for 12% of the time, Pallas kernels for 0%

commit v1 on v0

--- a/solution.py
+++ b/solution.py
@@ -66,11 +66,34 @@
     second_shrink,
     second_norms,
 ):
+
+    def lay_the_orders(original, dim_i):
+        mesh_dim = "fsdp"
+        n_dev_all = lax.axis_size(mesh_dim)
+        inbox = []
+        for c in range(n_dev_all):
+            inbox.append((c, (c + 1) % n_dev_all))
+        ledger = []
+        for c in range(n_dev_all):
+            ledger.append((c, (c - 1) % n_dev_all))
+        part_now, f_now = ([original], [original])
+        for _ in range(n_dev_all // 2):
+            near = lax.ppermute(part_now[-1], mesh_dim, inbox)
+            part_now.append(near)
+        for _ in range((n_dev_all - 1) // 2):
+            f_next = lax.ppermute(f_now[-1], mesh_dim, ledger)
+            f_now.append(f_next)
+        piece_now = jnp.concatenate([*part_now[::-1], *f_now[1:]], axis=dim_i)
+        opened = lax.axis_index(mesh_dim)
+        return jnp.roll(
+            piece_now, shift=(opened - n_dev_all // 2) * original.shape[dim_i], axis=dim_i
+        )
+
     whole_attend, whole_mixing, whole_expand, whole_shrink, whole_norms = (
         lax.all_gather(w_attend, "fsdp", axis=0, tiled=True),
         lax.all_gather(w_mixing, "fsdp", axis=0, tiled=True),
         lax.all_gather(w_expand, "fsdp", axis=0, tiled=True),
-        lax.all_gather(w_shrink, "fsdp", axis=0, tiled=True),
+        lay_the_orders(w_shrink, 0),
         lax.all_gather(w_norms, "fsdp", axis=1, tiled=True),
     )
     seqs, local, width = tokens.shape

time: 1210 us -> 1150 us (0.950)
  waiting for transfers between devices: 833 us -> 763 us
  local copies, waits for them, and re-layouts: 87.7 us -> 105 us
    all_gather x1, waiting for transfers between devices: 70.6 us -> 0.02 us  [shards(): lax.all_gather(values_own, 'ctx', axis=1, tiled=True)]
    ppermute x0 -> x3, waiting for transfers between devices: none -> 70.6 us  [the longest x2 70.6 us: lay_the_orders(): near = lax.ppermute(part_now[-1], mesh_dim, inbox)]
    all_gather x1 -> x0, waiting for transfers between devices: 49.5 us -> none  [shards(): lax.all_gather(w_shrink, 'fsdp', axis=0, tiled=True)]
    all_gather x1, waiting for transfers between devices: 68 us -> 50.1 us  [shards(): lax.all_gather(keys_own, 'ctx', axis=1, tiled=True)]
    unnamed x69 -> x84, local copies, waits for them, and re-layouts: 20.7 us -> 35.8 us
  transfers between devices with their start and end apart: 14 -> 16, of which waited for: 12 -> 12; matrix products, arithmetic and copies ran while one was open for 12% -> 12% of each run, Pallas kernels for 0% -> 0%
where the time goes in v1:
time: 1150 us
  waiting for transfers between devices  763 us (66%)
  matrix products  165 us (14%)
  local copies, waits for them, and re-layouts  105 us (9%)
  other arithmetic  68.2 us (6%)
  blocking collectives  28.1 us (2%)
  between operations  14.8 us (1%)
    psum x1, waiting for transfers between devices, shards(): lax.psum(owned_attend.astype(jnp.bfloat16), 'ctx').astype(jnp.float32)  196 us
    reduce_scatter x1, waiting for transfers between devices, shards(): lax.psum_scatter(grad_keys_all.astype(jnp.bfloat16), 'ctx', scatter_dimen...  92.8 us
    reduce_scatter x1, waiting for transfers between devices, shards(): lax.psum_scatter(grad_expand.astype(jnp.bfloat16), 'fsdp', scatter_dimens...  74.5 us
    reduce_scatter x1, waiting for transfers between devices, shards(): lax.psum_scatter(grad_shrink.astype(jnp.bfloat16), 'fsdp', scatter_dimens...  74.2 us
    ppermute x2, waiting for transfers between devices, lay_the_orders(): near = lax.ppermute(part_now[-1], mesh_dim, inbox)  70.6 us
    reduce_scatter x1, waiting for transfers between devices, shards(): lax.psum_scatter(grad_values_all.astype(jnp.bfloat16), 'ctx', scatter_dim...  65.4 us
    reduce_scatter x1, waiting for transfers between devices, shards(): lax.psum_scatter(grad_attend.astype(jnp.bfloat16), 'fsdp', scatter_dimens...  61.1 us
    dot_general x16, matrix products, group_scores(): jnp.einsum('sqhd,skhd->shqk', query_group, key_group, preferred_element_t...  56.6 us
  transfers between devices with their start and end apart: 16, of which 12 were waited for; matrix products, arithmetic and copies ran while one was open for 12% of the time, Pallas kernels for 0%

profile of v1, /device:TPU:0, one launch (start us, length us, event | category | flops | bytes accessed | tf_op | source)
XLA Modules:
  0.0 1147.5 jit_solution(10896209411157313139)
XLA Ops:
  8.0 6.3 all_gather.18
  16.8 41.9 %all-gather.8.cloned.1.call-done = bf16[1024,3072]{1,0:T(8,128)(2,1)} async-done(((bf16[256,3072]{1,0:T(8,128)(2,1)}), bf16[1024,3072]{1,0:T(8,128)(2,1)}) %all-gather.8.cloned.1.call-update) | async-done | bytes 6291472 | tf_op jit(solution)/shard_map/all_gather | solution.py:93
  58.7 4.9 convolution_convert_fusion.3
  66.1 25.0 %collective-permute-done = bf16[1024,1024]{1,0:T(8,128)(2,1)} collective-permute-done((bf16[1024,1024]{1,0:T(8,128)(2,1)S(1)}, bf16[1024,1024]{1,0:T(8,128)(2,1)}, u32[]{:S(2)}, u32[]{:S(2)}) %collective-permute-start) | collective-permute-done | bytes 2097184 | tf_op jit(solution)/shard_map/ppermute | solution.py:81
  93.6 45.5 %collective-permute-done.1 = bf16[1024,1024]{1,0:T(8,128)(2,1)} collective-permute-done((bf16[1024,1024]{1,0:T(8,128)(2,1)}, bf16[1024,1024]{1,0:T(8,128)(2,1)}, u32[]{:S(2)}, u32[]{:S(2)}) %collective-permute-start.1) | collective-permute-done | bytes 2097184 | tf_op jit(solution)/shard_map/ppermute | solution.py:81
  150.2 5.7 copy-done.28
  156.2 6.5 copy.48
  162.6 50.1 %all-gather.16.cloned.1.call-done = bf16[2048,1024]{1,0:T(8,128)(2,1)} async-done(((bf16[256,1024]{1,0:T(8,128)(2,1)}), bf16[2048,1024]{1,0:T(8,128)(2,1)}) %all-gather.16.cloned.1.call-update) | async-done | bytes 4194320 | tf_op jit(solution)/shard_map/all_gather | solution.py:121
  212.8 6.4 copy.50
  219.3 74.3 %while.34 = (s32[]{:T(128)}, bf16[1,256,1024]{1,2,0:T(8,128)(2,1)S(1)}, f32[1,16,256]{2,1,0:T(8,128)S(1)}, bf16[1,2048,1024]{1,2,0:T(8,128)(2,1)}, bf16[1,256,10...) while((s32[]{:T(128)}, ...), condition=%wide.region_5.6_spmd.clone, body=%wide.region_2.5_spmd.clone.sunk | while | flops 276332032 | bytes 33973524 | solution.py:160
  221.0 3.0 fusion.139
  224.1 3.1 exponential_reduce_fusion.2
  230.2 3.0 fusion.139
  233.2 3.1 exponential_reduce_fusion.2
  242.3 3.6 exponential_reduce_fusion.2
  267.9 3.0 fusion.139
  270.9 3.1 exponential_reduce_fusion.2
  277.0 3.0 fusion.139
  286.2 3.0 fusion.139
  297.1 6.0 fusion.85
  303.1 9.5 fusion.27
  324.4 120.1 %while.35 = (s32[]{:T(128)}, bf16[1,256,1024]{1,2,0:T(8,128)(2,1)}, bf16[1,2048,1024]{1,2,0:T(8,128)(2,1)}, bf16[1,2048,1024]{1,2,0:T(8,128)(2,1)}, bf16[1,2048,...) while((s32[]{:T(128)}, bf16[1,256,1024]{1,2,0:T(8,128)(2,1)}, ...), condition=%wide.region_12.13_spmd.clone, body=%wide.region_10.12_spmd.clone.sunk | while | flops 681639424 | bytes 56970552 | solution.py:236
  331.5 4.0 multiply_reduce_fusion.5
  346.5 4.0 multiply_reduce_fusion.5
  361.5 4.0 multiply_reduce_fusion.5
  376.6 4.0 multiply_reduce_fusion.5
  391.6 4.0 multiply_reduce_fusion.5
  406.6 4.0 multiply_reduce_fusion.5
  421.6 4.0 multiply_reduce_fusion.5
  436.6 4.0 multiply_reduce_fusion.5
  445.6 3.1 convolution_convert_fusion.4
  448.9 7.6 convolution_convert_fusion.1
  457.5 8.5 convolution_convert_fusion
  466.1 65.4 %reduce-scatter.12.cloned.1.call-done = bf16[1,256,1024]{1,2,0:T(8,128)(2,1)} async-done(((bf16[1,2048,1024]{1,2,0:T(8,128)(2,1)}), bf16[1,256,1024]{1,2,0:T(8,128)(2,1)}) %reduce-scatter.12.cloned.1.call-update) | async-done | bytes 524304 | tf_op jit(solution)/shard_map/reduce_scatter | solution.py:250
  531.5 92.8 %reduce-scatter.10.cloned.1.call-done = bf16[1,256,1024]{1,2,0:T(8,128)(2,1)} async-done(((bf16[1,2048,1024]{1,2,0:T(8,128)(2,1)}), bf16[1,256,1024]{1,2,0:T(8,128)(2,1)}) %reduce-scatter.10.cloned.1.call-update) | async-done | bytes 524304 | tf_op jit(solution)/shard_map/reduce_scatter | solution.py:247
  624.3 5.8 convolution_convert_fusion.2
  630.2 5.4 fusion.54
  638.5 20.1 %reduce-scatter.16.cloned.1.call-done = bf16[256,1024]{1,0:T(8,128)(2,1)} async-done(((bf16[1024,1024]{1,0:T(8,128)(2,1)}), bf16[256,1024]{1,0:T(8,128)(2,1)}) %reduce-scatter.16.cloned.1.call-update) | async-done | bytes 524304 | tf_op jit(solution)/shard_map/reduce_scatter | solution.py:271
  658.6 74.5 %reduce-scatter.18.cloned.1.call-done = bf16[256,4096]{1,0:T(8,128)(2,1)} async-done(((bf16[1024,4096]{1,0:T(8,128)(2,1)}), bf16[256,4096]{1,0:T(8,128)(2,1)}) %reduce-scatter.18.cloned.1.call-update) | async-done | bytes 2097168 | tf_op jit(solution)/shard_map/reduce_scatter | solution.py:274
  733.1 74.2 %reduce-scatter.20.cloned.1.call-done = bf16[1024,1024]{1,0:T(8,128)(2,1)} async-done(((bf16[4096,1024]{1,0:T(8,128)(2,1)}), bf16[1024,1024]{1,0:T(8,128)(2,1)}) %reduce-scatter.20.cloned.1.call-update) | async-done | bytes 2097168 | tf_op jit(solution)/shard_map/reduce_scatter | solution.py:277
  807.3 61.1 %reduce-scatter.14.cloned.1.call-done = bf16[256,3072]{1,0:T(8,128)(2,1)} async-done(((bf16[1024,3072]{1,0:T(8,128)(2,1)}), bf16[256,3072]{1,0:T(8,128)(2,1)}) %reduce-scatter.14.cloned.1.call-update) | async-done | bytes 1572880 | tf_op jit(solution)/shard_map/reduce_scatter | solution.py:268
  868.4 8.3 fusion.44
  878.2 13.1 %reduce-scatter.22.cloned.1.call-done = bf16[256,4]{1,0:T(8,128)(2,1)} async-done(((bf16[1024,4]{1,0:T(8,128)(2,1)}), bf16[256,4]{1,0:T(8,128)(2,1)}) %reduce-scatter.22.cloned.1.call-update) | async-done | bytes 2064
  892.3 21.8 %psum.39 = bf16[4,256]{1,0:T(4,128)(2,1)S(1)} all-reduce(bf16[4,256]{1,0:T(4,128)(2,1)S(1)} %copy.58), channel_id=1, replica_groups=mesh['fsdp'=4,'ctx'=8] {'ctx'}, use_global_device_ids=true, to_apply=%region_30.31 | all-reduce | flops 1024 | bytes 4096 | tf_op jit(solution)/shard_map/psum | solution.py:289
  914.7 196.3 %all-reduce.3.cloned.1.call-done = (bf16[256,3072]{1,0:T(8,128)(2,1)}, bf16[256,1024]{1,0:T(8,128)(2,1)}, bf16[256,4096]{1,0:T(8,128)(2,1)}, bf16[1024,1024]{1,0:T(8,128)(2,1)}) async-done(((bf16[256,3072]{1,0:T(8,128)(2,1)}, bf16[256,1024]{1,0:T(8,128)(2,1)}, bf16[256,4096]{1,0:T(8,128)(2,1)}, bf16[1024,1024]{1,0:T(8,128)(2,1)}), (bf16[256,3072]{1,0:T(8,128)(2,1)}, bf16[256,1024]{1,0:T(8,128)(2,1)}, ...) | async-done | bytes 6291472 | tf_op jit(solution)/shard_map/psum | solution.py:285
  1111.0 8.7 add_multiply_fusion.2
  1124.1 9.8 add_multiply_fusion.1
  1134.0 6.8 add_multiply_fusion
  (353 shorter events, 180.3 us)
Async XLA Ops:
  7.2 51.5 %all-gather.8.cloned.1.call-start = ((), (), s32[]{:S(2)}) async-start(), calls=%async_computation.7 | async-start | bytes 7864320 | tf_op jit(solution)/shard_map/all_gather | solution.py:93
  7.9 148.3 %all-gather.14.cloned.1.call-start = ((), (), s32[]{:S(2)}) async-start(), calls=%async_computation.16 | async-start | bytes 4718592 | tf_op jit(solution)/shard_map/all_gather | solution.py:122
  16.8 46.8 %copy-start.29 = (f32[256]{0:T(256)}, f32[256]{0:T(256)S(1)}, u32[]{:S(2)}) copy-start(f32[256]{0:T(256)S(1)} %fusion.53) | copy-start | bytes 3076
  63.6 29.7 %copy-start.34 = (s32[1,16]{1,0:T(1,128)S(1)}, s32[1,16]{1,0:T(1,128)}, u32[]{:S(2)}) copy-start(s32[1,16]{1,0:T(1,128)} %param.24) | copy-start | bytes 196
  64.8 148.0 %all-gather.16.cloned.1.call-start = ((), (), s32[]{:S(2)}) async-start(), calls=%async_computation.17 | async-start | bytes 4718592 | tf_op jit(solution)/shard_map/all_gather | solution.py:121
  65.5 228.1 %all-gather.10.cloned.1.call-start = ((), (), s32[]{:S(2)}) async-start(), calls=%async_computation.8 | async-start | bytes 2621440 | tf_op jit(solution)/shard_map/all_gather | solution.py:94
  65.6 25.6 %collective-permute-start = (bf16[1024,1024]{1,0:T(8,128)(2,1)S(1)}, bf16[1024,1024]{1,0:T(8,128)(2,1)}, u32[]{:S(2)}, u32[]{:S(2)}) collective-permute-start(bf16[1024,1024]{1,0:T(8,128)(2,1)S(1)} %copy-done.2), channel_id=1, source_target_pairs={{0,8},{8,16},{16,24},{24,0},{1,9},{9,17},{17,25},{25,1},{2,10},{10... | collective-permute-start | bytes 6291464 | tf_op jit(solution)/shard_map/ppermute | solution.py:81
  66.1 231.0 %all-gather.12.cloned.1.call-start = ((), (), s32[]{:S(2)}) async-start(), calls=%async_computation.9 | async-start | bytes 10485760 | tf_op jit(solution)/shard_map/all_gather | solution.py:95
  91.2 47.9 %collective-permute-start.1 = (bf16[1024,1024]{1,0:T(8,128)(2,1)}, bf16[1024,1024]{1,0:T(8,128)(2,1)}, u32[]{:S(2)}, u32[]{:S(2)}) collective-permute-start(bf16[1024,1024]{1,0:T(8,128)(2,1)} %collective-permute-done), channel_id=1, source_target_pairs={{0,8},{8,16},{16,24},{24,0},{1,9},{9,17},{17,25},{25,1},{2,10},{10... | collective-permute-start | bytes 6291464 | tf_op jit(solution)/shard_map/ppermute | solution.py:81
  91.2 51.6 %collective-permute-start.2 = (bf16[1024,1024]{1,0:T(8,128)(2,1)S(1)}, bf16[1024,1024]{1,0:T(8,128)(2,1)}, u32[]{:S(2)}, u32[]{:S(2)}) collective-permute-start(bf16[1024,1024]{1,0:T(8,128)(2,1)S(1)} %copy-done.2), channel_id=1, source_target_pairs={{0,24},{8,0},{16,8},{24,16},{1,25},{9,1},{17,9},{25,17},{2,26},{10... | collective-permute-start | bytes 6291464 | tf_op jit(solution)/shard_map/ppermute | solution.py:84
  92.9 438.6 %reduce-scatter.12.cloned.1.call-start = ((), (), s32[]{:S(2)}) async-start(), calls=%async_computation.11 | async-start | bytes 4718592 | tf_op jit(solution)/shard_map/reduce_scatter | solution.py:250
  150.2 5.7 copy-start.28
  219.3 75.1 %copy-start.4 = (bf16[1,256,1024]{2,1,0:T(8,128)(2,1)S(1)}, bf16[1,256,1024]{2,1,0:T(8,128)(2,1)}, u32[]{:S(2)}) copy-start(bf16[1,256,1024]{2,1,0:T(8,128)(2,1)} %param.22) | copy-start | bytes 1572868
  242.3 4.7 copy-start
  293.6 9.5 copy-start.7
  297.1 6.0 copy-start.20
  297.1 15.6 %slice-start = ((s8[8388608]{0:T(1024)(128)(4,1)}), s8[4194304]{0:T(1024)(128)(4,1)S(1)}, s32[]{:S(2)}) async-start(s8[8388608]{0:T(1024)(128)(4,1)} %bitcast.232), calls=%async_computation.20 | async-start | bytes 8388608
  303.1 9.6 copy-start.35
  303.1 9.6 slice-start.1
  317.0 7.4 copy-start.23
  331.5 4.0 copy-start.1
  346.5 4.0 copy-start.1
  376.6 4.0 copy-start.1
  444.5 179.7 %reduce-scatter.10.cloned.1.call-start = ((), (), s32[]{:S(2)}) async-start(), calls=%async_computation.10 | async-start | bytes 4718592 | tf_op jit(solution)/shard_map/reduce_scatter | solution.py:247
  445.3 213.3 %reduce-scatter.16.cloned.1.call-start = ((), (), s32[]{:S(2)}) async-start(), calls=%async_computation.13 | async-start | bytes 2621440 | tf_op jit(solution)/shard_map/reduce_scatter | solution.py:271
  448.7 284.4 %reduce-scatter.18.cloned.1.call-start = ((), (), s32[]{:S(2)}) async-start(), calls=%async_computation.14 | async-start | bytes 10485760 | tf_op jit(solution)/shard_map/reduce_scatter | solution.py:274
  456.5 350.8 %reduce-scatter.20.cloned.1.call-start = ((), (), s32[]{:S(2)}) async-start(), calls=%async_computation.15 | async-start | bytes 10485760 | tf_op jit(solution)/shard_map/reduce_scatter | solution.py:277
  466.0 158.3 %copy-start.27 = (bf16[1,256,1024]{1,2,0:T(8,128)(2,1)S(1)}, bf16[1,256,1024]{1,2,0:T(8,128)(2,1)}, u32[]{:S(2)}) copy-start(bf16[1,256,1024]{1,2,0:T(8,128)(2,1)} %get-tuple-element.320) | copy-start | bytes 1572868
  466.0 402.4 %reduce-scatter.14.cloned.1.call-start = ((), (), s32[]{:S(2)}) async-start(), calls=%async_computation.12 | async-start | bytes 7864320 | tf_op jit(solution)/shard_map/reduce_scatter | solution.py:268
  630.1 261.2 %reduce-scatter.22.cloned.1.call-start = ((), (), s32[]{:S(2)}) async-start(), calls=%async_computation.18 | async-start | bytes 327680
  630.2 5.5 copy-start.30
  638.2 472.8 %all-reduce.3.cloned.1.call-start = ((), (), s32[]{:S(2)}) async-start(), calls=%async_computation.19 | async-start | bytes 12582912 | tf_op jit(solution)/shard_map/psum | solution.py:285
  868.4 8.3 copy-start.14
  868.4 8.3 copy-start.22
  876.7 37.4 %copy-start.31 = (bf16[4,256]{1,0:T(4,128)(2,1)S(1)}, bf16[4,256]{1,0:T(4,128)(2,1)}, u32[]{:S(2)}) copy-start(bf16[4,256]{1,0:T(4,128)(2,1)} %param.29) | copy-start | bytes 6148
  876.7 37.4 %copy-start.32 = (f32[4,256]{1,0:T(4,128)S(1)}, f32[4,256]{1,0:T(4,128)}, u32[]{:S(2)}) copy-start(f32[4,256]{1,0:T(4,128)} %param.34) | copy-start | bytes 12292
  876.7 37.4 %copy-start.33 = (f32[4,256]{1,0:T(4,128)S(1)}, f32[4,256]{1,0:T(4,128)}, u32[]{:S(2)}) copy-start(f32[4,256]{1,0:T(4,128)} %param.39) | copy-start | bytes 12292
  876.7 234.3 %copy-start.6 = (bf16[256,3072]{1,0:T(8,128)(2,1)S(1)}, bf16[256,3072]{1,0:T(8,128)(2,1)}, u32[]{:S(2)}) copy-start(bf16[256,3072]{1,0:T(8,128)(2,1)} %param.25) | copy-start | bytes 4718596
  1111.0 8.7 copy-start.17
  1111.0 8.7 copy-start.24
  1111.0 8.7 copy-start.25
  1111.0 8.7 copy-start.26
  1111.0 11.2 copy-start.10
  1119.7 4.4 copy-start.9
  1124.1 9.9 copy-start.3
  1124.1 9.9 copy-start.11
  1124.1 9.9 copy-start.12
  1124.1 9.9 copy-start.16
  (20 other events, 57.3 us)
Sparse Core Ops, SparseCore 0:
  9.6 49.0 all-gather.7
  64.9 73.4 all-gather.13
  141.1 71.6 all-gather.15
  214.2 20.8 all-gather.9
  236.5 58.2 all-gather.11
  444.7 86.7 reduce-scatter.11
  536.1 88.0 reduce-scatter.9
  627.4 31.1 reduce-scatter.15
  661.3 71.7 reduce-scatter.17
  735.5 71.7 reduce-scatter.19
  810.0 58.3 reduce-scatter.13
  871.3 20.0 reduce-scatter.21
  896.4 214.5 all-reduce.2
